TPU v7x, 128 devices: a whole 4x4x4 slice. The times are simulated.
128 devices in a mesh: blk: 16 (over x_hi, y, core), bal: 8 (over x_lo, z).
Axes of the slice: x: 4 (x_hi: 2, x_lo: 2; x = x_hi * 2 + x_lo), y: 4, z: 4, core: 2. Of those that a mesh axis runs over, the one named last changes fastest.
Arguments:
- features: bfloat16 [131072, 512], P('blk', 'bal'), may hold values from -6 to 6
- tile_values: bfloat16 [16, 16, 32, 128, 128], P('blk'), may hold values from 0.049804688 to 1
- tile_rows: int32 [16, 16, 32], P('blk'), may hold values from 0 to 63
- tile_cols: int32 [16, 16, 32], P('blk'), may hold values from 0 to 63
- tile_counts: int32 [16, 16], P('blk'), may hold values from 8 to 32, as said below
- w_self: bfloat16 [512, 512], replicated, may hold values from -0.25 to 0.25
- w_neigh: bfloat16 [512, 512], replicated, may hold values from -6 to 6
- bias: float32 [512], replicated, may hold values from -3 to 3
- part_map: int32 [16, 64], P('blk'), may hold values from 0 to 7, as said below
Outputs:
- next_rows: bfloat16 [16, 8, 2048, 512], P('blk', 'bal')
Inputs may be any that keep to these rules, and one draw needn't show every extreme that they name: `tile_counts`: live slots of one pair of vertex blocks; the most, 32, is reached by some pair in every draw. `part_map`: within one block of vertex rows at most 16 tiles go to any one value, and exactly 16 to some value.
All inputs are finite; a program needn't handle non-finite values.
Results may differ from a plain program's by a relative error of at most 0.0036.
Values may be sent and summed in bfloat16 or wider, within the bound.
No kernel may reach another device: no remote copies, remote signals or barrier semaphores. Data moves between devices by JAX's collectives and lax.ppermute only.
A program may use at most 128 MiB of HBM per device.

v0:
```python
import jax
import jax.numpy as jnp
from jax import lax
from jax.sharding import PartitionSpec as P

TILE = 128


def from_behind(block, axis, distance):
    devices = range(lax.axis_size(axis))
    route = [((i - distance) % len(devices), i) for i in devices]
    return lax.ppermute(block, axis, route)


def advance(block, steps_by):
    return from_behind(block, "blk", steps_by)


def on_device(
    features, tile_values, tile_rows, tile_cols, tile_counts, w_self, w_neigh, bias, part_map
):
    n_blk = lax.axis_size("blk")
    n_bal = lax.axis_size("bal")
    here = lax.axis_index("blk")
    column = lax.axis_index("bal")
    width = features.shape[1]
    tiles_per = part_map.shape[1]
    values = tile_values[0]
    rows_idx = tile_rows[0]
    cols_idx = tile_cols[0]
    counts = tile_counts[0]
    slots = values.shape[1]
    live = jnp.arange(slots)[None, :] < counts[:, None]
    row_hot = (
        (rows_idx[:, :, None] == jnp.arange(tiles_per)[None, None, :]) & live[:, :, None]
    ).astype(jnp.float32)
    row_mass = jnp.einsum(
        "csij,j->csi", values, jnp.ones((TILE,), jnp.bfloat16), preferred_element_type=jnp.float32
    )
    degree = 1.0 + jnp.einsum("cst,csi->ti", row_hot, row_mass, precision=lax.Precision.HIGHEST)

    def absorb(total, block, source):
        tiles = block.reshape(tiles_per, TILE, width)
        vals = lax.dynamic_index_in_dim(values, source, 0, keepdims=False)
        picks = lax.dynamic_index_in_dim(cols_idx, source, 0, keepdims=False)
        targets = lax.dynamic_index_in_dim(rows_idx, source, 0, keepdims=False)
        alive = lax.dynamic_index_in_dim(live, source, 0, keepdims=False)
        gathered = jnp.take(tiles, picks, axis=0)
        prod = jnp.einsum("sij,sjf->sif", vals, gathered, preferred_element_type=jnp.float32)
        masked = jnp.where(alive[:, None, None], prod, 0.0)
        return total.at[targets].add(masked)

    empty = jnp.zeros((tiles_per, TILE, width), jnp.float32)

    def step_one(index, carry):
        total, block = carry
        total = absorb(total, block, (here - index) % n_blk)
        block = advance(block, 1)
        return (total, block)

    total, block = lax.fori_loop(0, n_blk - 1, step_one, (empty, features))
    total = absorb(total, block, (here - (n_blk - 1)) % n_blk)
    mean_agg = (total / degree[:, :, None]).astype(jnp.bfloat16).reshape(tiles_per * TILE, width)
    capacity = 2 * tiles_per // n_bal
    mapping = part_map[0]
    dest_hot = (mapping[:, None] == jnp.arange(n_bal)[None, :]).astype(jnp.int32)
    ranks = jnp.cumsum(dest_hot, axis=0) - dest_hot
    place = mapping * capacity + jnp.sum(ranks * dest_hot, axis=1)
    select = (jnp.arange(n_bal * capacity)[:, None] == place[None, :]).astype(jnp.bfloat16)
    col_start = column * width
    zeros_out = jnp.zeros((tiles_per * TILE, width), jnp.float32)
    carry = zeros_out
    mean_piece = lax.all_gather(mean_agg, "bal", axis=1, tiled=True)
    feat_piece = lax.all_gather(features, "bal", axis=1, tiled=True)
    count = mean_piece.shape[1]
    neigh_part = lax.dynamic_slice(w_neigh, (0, col_start), (count, width))
    self_part = lax.dynamic_slice(w_self, (0, col_start), (count, width))
    carry = jnp.dot(mean_piece, neigh_part, preferred_element_type=jnp.float32)
    pre = carry + jnp.dot(feat_piece, self_part, preferred_element_type=jnp.float32)
    pre = pre + lax.dynamic_slice_in_dim(bias, col_start, width)
    hidden = jnp.maximum(pre, 0.0).astype(jnp.bfloat16)
    tiles = hidden.reshape(tiles_per, TILE, width)
    placed = jnp.einsum("kt,tif->kif", select, tiles, preferred_element_type=jnp.float32)
    result = lax.all_to_all(
        placed.astype(jnp.bfloat16).reshape(n_bal, capacity * TILE, width),
        "bal",
        split_axis=0,
        concat_axis=2,
        tiled=True,
    )
    return result[None]


def solution(mesh):
    placed = (
        P("blk", "bal"),
        P("blk", None, None, None, None),
        P("blk", None, None),
        P("blk", None, None),
        P("blk", None),
        P(),
        P(),
        P(),
        P("blk", None),
    )
    return jax.shard_map(
        on_device,
        mesh=mesh,
        in_specs=placed,
        out_specs=P("blk", "bal", None, None),
        check_vma=False,
    )
```

profile of v0, /device:TPU:0, one launch (start us, length us, event | category | flops | bytes accessed | tf_op | source)
XLA Modules:
  0.0 528.4 jit_solution(13366378268195812882)
XLA Ops:
  12.0 343.1 %while.17 = (s32[]{:T(128)}, f32[64,128,64]{1,2,0:T(8,128)}, bf16[8192,64]{0,1:T(8,128)(2,1)}, s32[]{:T(128)}, s32[16,32]{1,0:T(8,128)S(1)}, /*index=5*/pred[16,...) while((s32[]{:T(128)}, f32[64,128,64]{1,2,0:T(8,128)}, ...), condition=%wide.region_4.6_spmd, body=%wide.region_2.5_spmd.sunk | while | flops 67896624 | bytes 15209832 | solution.py:61
  17.0 4.9 scatter_fusion
  21.9 20.0 %collective-permute-done = bf16[8192,64]{0,1:T(8,128)(2,1)} collective-permute-done((bf16[8192,64]{0,1:T(8,128)(2,1)S(1)}, bf16[8192,64]{0,1:T(8,128)(2,1)}, u32[]{:S(2)}, u32[]{:S(2)}) %collective-permute-start) | collective-permute-done | bytes 1048608 | tf_op jit(solution)/shard_map/while/body/eval_jaxpr/ppermute | solution.py:12
  47.0 4.8 scatter_fusion
  51.8 31.8 %collective-permute-done = bf16[8192,64]{0,1:T(8,128)(2,1)} collective-permute-done((bf16[8192,64]{0,1:T(8,128)(2,1)S(1)}, bf16[8192,64]{0,1:T(8,128)(2,1)}, u32[]{:S(2)}, u32[]{:S(2)}) %collective-permute-start) | collective-permute-done | bytes 1048608 | tf_op jit(solution)/shard_map/while/body/eval_jaxpr/ppermute | solution.py:12
  88.5 4.8 scatter_fusion
  93.3 31.8 %collective-permute-done = bf16[8192,64]{0,1:T(8,128)(2,1)} collective-permute-done((bf16[8192,64]{0,1:T(8,128)(2,1)S(1)}, bf16[8192,64]{0,1:T(8,128)(2,1)}, u32[]{:S(2)}, u32[]{:S(2)}) %collective-permute-start) | collective-permute-done | bytes 1048608 | tf_op jit(solution)/shard_map/while/body/eval_jaxpr/ppermute | solution.py:12
  130.2 4.8 scatter_fusion
  134.9 9.4 %collective-permute-done = bf16[8192,64]{0,1:T(8,128)(2,1)} collective-permute-done((bf16[8192,64]{0,1:T(8,128)(2,1)S(1)}, bf16[8192,64]{0,1:T(8,128)(2,1)}, u32[]{:S(2)}, u32[]{:S(2)}) %collective-permute-start) | collective-permute-done | bytes 1048608 | tf_op jit(solution)/shard_map/while/body/eval_jaxpr/ppermute | solution.py:12
  149.3 4.8 scatter_fusion
  154.1 9.4 %collective-permute-done = bf16[8192,64]{0,1:T(8,128)(2,1)} collective-permute-done((bf16[8192,64]{0,1:T(8,128)(2,1)S(1)}, bf16[8192,64]{0,1:T(8,128)(2,1)}, u32[]{:S(2)}, u32[]{:S(2)}) %collective-permute-start) | collective-permute-done | bytes 1048608 | tf_op jit(solution)/shard_map/while/body/eval_jaxpr/ppermute | solution.py:12
  168.5 4.8 scatter_fusion
  173.3 9.4 %collective-permute-done = bf16[8192,64]{0,1:T(8,128)(2,1)} collective-permute-done((bf16[8192,64]{0,1:T(8,128)(2,1)S(1)}, bf16[8192,64]{0,1:T(8,128)(2,1)}, u32[]{:S(2)}, u32[]{:S(2)}) %collective-permute-start) | collective-permute-done | bytes 1048608 | tf_op jit(solution)/shard_map/while/body/eval_jaxpr/ppermute | solution.py:12
  187.7 4.8 scatter_fusion
  192.4 9.4 %collective-permute-done = bf16[8192,64]{0,1:T(8,128)(2,1)} collective-permute-done((bf16[8192,64]{0,1:T(8,128)(2,1)S(1)}, bf16[8192,64]{0,1:T(8,128)(2,1)}, u32[]{:S(2)}, u32[]{:S(2)}) %collective-permute-start) | collective-permute-done | bytes 1048608 | tf_op jit(solution)/shard_map/while/body/eval_jaxpr/ppermute | solution.py:12
  206.8 4.8 scatter_fusion
  211.6 9.4 %collective-permute-done = bf16[8192,64]{0,1:T(8,128)(2,1)} collective-permute-done((bf16[8192,64]{0,1:T(8,128)(2,1)S(1)}, bf16[8192,64]{0,1:T(8,128)(2,1)}, u32[]{:S(2)}, u32[]{:S(2)}) %collective-permute-start) | collective-permute-done | bytes 1048608 | tf_op jit(solution)/shard_map/while/body/eval_jaxpr/ppermute | solution.py:12
  226.0 4.8 scatter_fusion
  230.8 9.4 %collective-permute-done = bf16[8192,64]{0,1:T(8,128)(2,1)} collective-permute-done((bf16[8192,64]{0,1:T(8,128)(2,1)S(1)}, bf16[8192,64]{0,1:T(8,128)(2,1)}, u32[]{:S(2)}, u32[]{:S(2)}) %collective-permute-start) | collective-permute-done | bytes 1048608 | tf_op jit(solution)/shard_map/while/body/eval_jaxpr/ppermute | solution.py:12
  245.2 4.8 scatter_fusion
  249.9 9.4 %collective-permute-done = bf16[8192,64]{0,1:T(8,128)(2,1)} collective-permute-done((bf16[8192,64]{0,1:T(8,128)(2,1)S(1)}, bf16[8192,64]{0,1:T(8,128)(2,1)}, u32[]{:S(2)}, u32[]{:S(2)}) %collective-permute-start) | collective-permute-done | bytes 1048608 | tf_op jit(solution)/shard_map/while/body/eval_jaxpr/ppermute | solution.py:12
  264.3 4.8 scatter_fusion
  269.1 9.4 %collective-permute-done = bf16[8192,64]{0,1:T(8,128)(2,1)} collective-permute-done((bf16[8192,64]{0,1:T(8,128)(2,1)S(1)}, bf16[8192,64]{0,1:T(8,128)(2,1)}, u32[]{:S(2)}, u32[]{:S(2)}) %collective-permute-start) | collective-permute-done | bytes 1048608 | tf_op jit(solution)/shard_map/while/body/eval_jaxpr/ppermute | solution.py:12
  288.3 9.4 %collective-permute-done = bf16[8192,64]{0,1:T(8,128)(2,1)} collective-permute-done((bf16[8192,64]{0,1:T(8,128)(2,1)S(1)}, bf16[8192,64]{0,1:T(8,128)(2,1)}, u32[]{:S(2)}, u32[]{:S(2)}) %collective-permute-start) | collective-permute-done | bytes 1048608 | tf_op jit(solution)/shard_map/while/body/eval_jaxpr/ppermute | solution.py:12
  307.4 9.4 %collective-permute-done = bf16[8192,64]{0,1:T(8,128)(2,1)} collective-permute-done((bf16[8192,64]{0,1:T(8,128)(2,1)S(1)}, bf16[8192,64]{0,1:T(8,128)(2,1)}, u32[]{:S(2)}, u32[]{:S(2)}) %collective-permute-start) | collective-permute-done | bytes 1048608 | tf_op jit(solution)/shard_map/while/body/eval_jaxpr/ppermute | solution.py:12
  326.6 9.4 %collective-permute-done = bf16[8192,64]{0,1:T(8,128)(2,1)} collective-permute-done((bf16[8192,64]{0,1:T(8,128)(2,1)S(1)}, bf16[8192,64]{0,1:T(8,128)(2,1)}, u32[]{:S(2)}, u32[]{:S(2)}) %collective-permute-start) | collective-permute-done | bytes 1048608 | tf_op jit(solution)/shard_map/while/body/eval_jaxpr/ppermute | solution.py:12
  345.8 9.4 %collective-permute-done = bf16[8192,64]{0,1:T(8,128)(2,1)} collective-permute-done((bf16[8192,64]{0,1:T(8,128)(2,1)S(1)}, bf16[8192,64]{0,1:T(8,128)(2,1)}, u32[]{:S(2)}, u32[]{:S(2)}) %collective-permute-start) | collective-permute-done | bytes 1048608 | tf_op jit(solution)/shard_map/while/body/eval_jaxpr/ppermute | solution.py:12
  366.6 10.2 %fusion.38 = f32[1,16,32,128]{3,0,2,1:T(1,128)S(1)} fusion(bf16[1,16,32,128,128]{4,3,2,1,0:T(8,128)(2,1)} %bitcast.106), kind=kOutput, calls=%fused_computation.70 | convolution fusion | flops 16777216 | bytes 17039360 | tf_op jit(solution)/shard_map/csij,j->csi/dot_general | solution.py:37
  379.7 5.1 convolution_bitcast_fusion
  384.8 93.0 %all-gather.3.cloned.1.call-done = bf16[8192,512]{0,1:T(8,128)(2,1)} async-done(((bf16[8192,64]{0,1:T(8,128)(2,1)}), bf16[8192,512]{0,1:T(8,128)(2,1)}) %all-gather.3.cloned.1.call-update) | async-done | bytes 8388624 | tf_op jit(solution)/shard_map/all_gather | solution.py:73
  477.8 5.2 fusion.13
  489.1 29.9 %all_to_all.15 = bf16[8,2048,64]{1,2,0:T(8,128)(2,1)S(1)} all-to-all(bf16[8,2048,64]{1,2,0:T(8,128)(2,1)S(1)} %copy.17), channel_id=1, replica_groups=mesh['blk'=16,'bal'=8] {'bal'}, dimensions={0} | all-to-all | bytes 4194304 | tf_op jit(solution)/shard_map/all_to_all | solution.py:84
  (177 shorter events, 122.0 us)
Async XLA Ops:
  6.5 373.1 %copy-start = (bf16[512,512]{1,0:T(8,128)(2,1)S(1)}, bf16[512,512]{1,0:T(8,128)(2,1)}, u32[]{:S(2)}) copy-start(bf16[512,512]{1,0:T(8,128)(2,1)} %param.18) | copy-start | bytes 1572868
  6.5 3.1 copy-start.3
  6.5 373.1 %all-gather.5.cloned.1.call-start = ((), (), s32[]{:S(2)}) async-start(), calls=%async_computation.2 | async-start | bytes 9437184 | tf_op jit(solution)/shard_map/all_gather | solution.py:74
  7.3 470.5 %all-gather.3.cloned.1.call-start = ((), (), s32[]{:S(2)}) async-start(), calls=%async_computation.1 | async-start | bytes 9437184 | tf_op jit(solution)/shard_map/all_gather | solution.py:73
  7.3 4.7 copy-start.4
  13.3 28.7 %collective-permute-start = (bf16[8192,64]{0,1:T(8,128)(2,1)S(1)}, bf16[8192,64]{0,1:T(8,128)(2,1)}, u32[]{:S(2)}, u32[]{:S(2)}) collective-permute-start(bf16[8192,64]{0,1:T(8,128)(2,1)S(1)} %copy.36), channel_id=1, source_target_pairs={{120,0},{0,8},{8,16},{16,24},{24,32},{32,40},{40,48},{48,56},{56,6... | collective-permute-start | bytes 3145736 | tf_op jit(solution)/shard_map/while/body/eval_jaxpr/ppermute | solution.py:12
  43.2 40.4 %collective-permute-start = (bf16[8192,64]{0,1:T(8,128)(2,1)S(1)}, bf16[8192,64]{0,1:T(8,128)(2,1)}, u32[]{:S(2)}, u32[]{:S(2)}) collective-permute-start(bf16[8192,64]{0,1:T(8,128)(2,1)S(1)} %copy.36), channel_id=1, source_target_pairs={{120,0},{0,8},{8,16},{16,24},{24,32},{32,40},{40,48},{48,56},{56,6... | collective-permute-start | bytes 3145736 | tf_op jit(solution)/shard_map/while/body/eval_jaxpr/ppermute | solution.py:12
  84.8 40.4 %collective-permute-start = (bf16[8192,64]{0,1:T(8,128)(2,1)S(1)}, bf16[8192,64]{0,1:T(8,128)(2,1)}, u32[]{:S(2)}, u32[]{:S(2)}) collective-permute-start(bf16[8192,64]{0,1:T(8,128)(2,1)S(1)} %copy.36), channel_id=1, source_target_pairs={{120,0},{0,8},{8,16},{16,24},{24,32},{32,40},{40,48},{48,56},{56,6... | collective-permute-start | bytes 3145736 | tf_op jit(solution)/shard_map/while/body/eval_jaxpr/ppermute | solution.py:12
  126.4 17.9 %collective-permute-start = (bf16[8192,64]{0,1:T(8,128)(2,1)S(1)}, bf16[8192,64]{0,1:T(8,128)(2,1)}, u32[]{:S(2)}, u32[]{:S(2)}) collective-permute-start(bf16[8192,64]{0,1:T(8,128)(2,1)S(1)} %copy.36), channel_id=1, source_target_pairs={{120,0},{0,8},{8,16},{16,24},{24,32},{32,40},{40,48},{48,56},{56,6... | collective-permute-start | bytes 3145736 | tf_op jit(solution)/shard_map/while/body/eval_jaxpr/ppermute | solution.py:12
  145.5 17.9 %collective-permute-start = (bf16[8192,64]{0,1:T(8,128)(2,1)S(1)}, bf16[8192,64]{0,1:T(8,128)(2,1)}, u32[]{:S(2)}, u32[]{:S(2)}) collective-permute-start(bf16[8192,64]{0,1:T(8,128)(2,1)S(1)} %copy.36), channel_id=1, source_target_pairs={{120,0},{0,8},{8,16},{16,24},{24,32},{32,40},{40,48},{48,56},{56,6... | collective-permute-start | bytes 3145736 | tf_op jit(solution)/shard_map/while/body/eval_jaxpr/ppermute | solution.py:12
  164.7 17.9 %collective-permute-start = (bf16[8192,64]{0,1:T(8,128)(2,1)S(1)}, bf16[8192,64]{0,1:T(8,128)(2,1)}, u32[]{:S(2)}, u32[]{:S(2)}) collective-permute-start(bf16[8192,64]{0,1:T(8,128)(2,1)S(1)} %copy.36), channel_id=1, source_target_pairs={{120,0},{0,8},{8,16},{16,24},{24,32},{32,40},{40,48},{48,56},{56,6... | collective-permute-start | bytes 3145736 | tf_op jit(solution)/shard_map/while/body/eval_jaxpr/ppermute | solution.py:12
  183.9 17.9 %collective-permute-start = (bf16[8192,64]{0,1:T(8,128)(2,1)S(1)}, bf16[8192,64]{0,1:T(8,128)(2,1)}, u32[]{:S(2)}, u32[]{:S(2)}) collective-permute-start(bf16[8192,64]{0,1:T(8,128)(2,1)S(1)} %copy.36), channel_id=1, source_target_pairs={{120,0},{0,8},{8,16},{16,24},{24,32},{32,40},{40,48},{48,56},{56,6... | collective-permute-start | bytes 3145736 | tf_op jit(solution)/shard_map/while/body/eval_jaxpr/ppermute | solution.py:12
  203.0 17.9 %collective-permute-start = (bf16[8192,64]{0,1:T(8,128)(2,1)S(1)}, bf16[8192,64]{0,1:T(8,128)(2,1)}, u32[]{:S(2)}, u32[]{:S(2)}) collective-permute-start(bf16[8192,64]{0,1:T(8,128)(2,1)S(1)} %copy.36), channel_id=1, source_target_pairs={{120,0},{0,8},{8,16},{16,24},{24,32},{32,40},{40,48},{48,56},{56,6... | collective-permute-start | bytes 3145736 | tf_op jit(solution)/shard_map/while/body/eval_jaxpr/ppermute | solution.py:12
  222.2 17.9 %collective-permute-start = (bf16[8192,64]{0,1:T(8,128)(2,1)S(1)}, bf16[8192,64]{0,1:T(8,128)(2,1)}, u32[]{:S(2)}, u32[]{:S(2)}) collective-permute-start(bf16[8192,64]{0,1:T(8,128)(2,1)S(1)} %copy.36), channel_id=1, source_target_pairs={{120,0},{0,8},{8,16},{16,24},{24,32},{32,40},{40,48},{48,56},{56,6... | collective-permute-start | bytes 3145736 | tf_op jit(solution)/shard_map/while/body/eval_jaxpr/ppermute | solution.py:12
  241.4 17.9 %collective-permute-start = (bf16[8192,64]{0,1:T(8,128)(2,1)S(1)}, bf16[8192,64]{0,1:T(8,128)(2,1)}, u32[]{:S(2)}, u32[]{:S(2)}) collective-permute-start(bf16[8192,64]{0,1:T(8,128)(2,1)S(1)} %copy.36), channel_id=1, source_target_pairs={{120,0},{0,8},{8,16},{16,24},{24,32},{32,40},{40,48},{48,56},{56,6... | collective-permute-start | bytes 3145736 | tf_op jit(solution)/shard_map/while/body/eval_jaxpr/ppermute | solution.py:12
  260.6 17.9 %collective-permute-start = (bf16[8192,64]{0,1:T(8,128)(2,1)S(1)}, bf16[8192,64]{0,1:T(8,128)(2,1)}, u32[]{:S(2)}, u32[]{:S(2)}) collective-permute-start(bf16[8192,64]{0,1:T(8,128)(2,1)S(1)} %copy.36), channel_id=1, source_target_pairs={{120,0},{0,8},{8,16},{16,24},{24,32},{32,40},{40,48},{48,56},{56,6... | collective-permute-start | bytes 3145736 | tf_op jit(solution)/shard_map/while/body/eval_jaxpr/ppermute | solution.py:12
  279.7 17.9 %collective-permute-start = (bf16[8192,64]{0,1:T(8,128)(2,1)S(1)}, bf16[8192,64]{0,1:T(8,128)(2,1)}, u32[]{:S(2)}, u32[]{:S(2)}) collective-permute-start(bf16[8192,64]{0,1:T(8,128)(2,1)S(1)} %copy.36), channel_id=1, source_target_pairs={{120,0},{0,8},{8,16},{16,24},{24,32},{32,40},{40,48},{48,56},{56,6... | collective-permute-start | bytes 3145736 | tf_op jit(solution)/shard_map/while/body/eval_jaxpr/ppermute | solution.py:12
  298.9 17.9 %collective-permute-start = (bf16[8192,64]{0,1:T(8,128)(2,1)S(1)}, bf16[8192,64]{0,1:T(8,128)(2,1)}, u32[]{:S(2)}, u32[]{:S(2)}) collective-permute-start(bf16[8192,64]{0,1:T(8,128)(2,1)S(1)} %copy.36), channel_id=1, source_target_pairs={{120,0},{0,8},{8,16},{16,24},{24,32},{32,40},{40,48},{48,56},{56,6... | collective-permute-start | bytes 3145736 | tf_op jit(solution)/shard_map/while/body/eval_jaxpr/ppermute | solution.py:12
  318.1 17.9 %collective-permute-start = (bf16[8192,64]{0,1:T(8,128)(2,1)S(1)}, bf16[8192,64]{0,1:T(8,128)(2,1)}, u32[]{:S(2)}, u32[]{:S(2)}) collective-permute-start(bf16[8192,64]{0,1:T(8,128)(2,1)S(1)} %copy.36), channel_id=1, source_target_pairs={{120,0},{0,8},{8,16},{16,24},{24,32},{32,40},{40,48},{48,56},{56,6... | collective-permute-start | bytes 3145736 | tf_op jit(solution)/shard_map/while/body/eval_jaxpr/ppermute | solution.py:12
  337.2 17.9 %collective-permute-start = (bf16[8192,64]{0,1:T(8,128)(2,1)S(1)}, bf16[8192,64]{0,1:T(8,128)(2,1)}, u32[]{:S(2)}, u32[]{:S(2)}) collective-permute-start(bf16[8192,64]{0,1:T(8,128)(2,1)S(1)} %copy.36), channel_id=1, source_target_pairs={{120,0},{0,8},{8,16},{16,24},{24,32},{32,40},{40,48},{48,56},{56,6... | collective-permute-start | bytes 3145736 | tf_op jit(solution)/shard_map/while/body/eval_jaxpr/ppermute | solution.py:12
  357.7 5.2 copy-start.1
  377.4 1.2 copy-start.2
Sparse Core Ops, SparseCore 0:
  9.0 94.5 all-gather.4
  378.6 99.1 all-gather.2
where the time goes:
time: 533 us; the launch traced here: 528 us
  waiting for transfers between devices  290 us (54%)
  other arithmetic  88.5 us (17%)
  matrix products  56 us (11%)
  local copies, waits for them, and re-layouts  49.7 us (9%)
  blocking collectives  29.9 us (6%)
  between operations  13.5 us (3%)
    ppermute x15, waiting for transfers between devices, from_behind(): return lax.ppermute(block, axis, route)  196 us
    all_gather x1, waiting for transfers between devices, on_device(): mean_piece = lax.all_gather(mean_agg, 'bal', axis=1, tiled=True)  93 us
    scatter-add x16, other arithmetic, absorb(): return total.at[targets].add(masked)  75.5 us
    dot_general x16, matrix products, absorb(): jnp.einsum('sij,sjf->sif', vals, gathered, preferred_element_type=jnp.flo...  34.2 us
    all_to_all x1, blocking collectives, on_device(): lax.all_to_all(placed.astype(jnp.bfloat16).reshape(n_bal, capacity * TILE...  29.9 us
    another operation x15, local copies, waits for them, and re-layouts  18.4 us
    gather x16, local copies, waits for them, and re-layouts, absorb(): gathered = jnp.take(tiles, picks, axis=0)  11.8 us
    and x16, other arithmetic, absorb(): gathered = jnp.take(tiles, picks, axis=0)  11.2 us
  transfers between devices with their start and end apart: 17, of which 16 were waited for; matrix products, arithmetic and copies ran while one was open for 34% of the time, Pallas kernels for 0%

commit v1 on v0

--- a/solution.py
+++ b/solution.py
@@ -70,8 +70,11 @@
     col_start = column * width
     zeros_out = jnp.zeros((tiles_per * TILE, width), jnp.float32)
     carry = zeros_out
-    mean_piece = lax.all_gather(mean_agg, "bal", axis=1, tiled=True)
-    feat_piece = lax.all_gather(features, "bal", axis=1, tiled=True)
+    mean_piece, feat_piece = jnp.split(
+        lax.all_gather(jnp.concatenate([mean_agg, features], axis=0), "bal", axis=1, tiled=True),
+        [mean_agg.shape[0]],
+        axis=0,
+    )
     count = mean_piece.shape[1]
     neigh_part = lax.dynamic_slice(w_neigh, (0, col_start), (count, width))
     self_part = lax.dynamic_slice(w_self, (0, col_start), (count, width))

time: 533 us -> 556 us (1.043)
  waiting for transfers between devices: 290 us -> 310 us
    all_gather x2 -> x1, waiting for transfers between devices: 93.1 us -> 169 us  [on_device(): lax.all_gather(jnp.concatenate([mean_agg, features], axis=0), 'bal', axis...]
    ppermute x15, waiting for transfers between devices: 196 us -> 141 us  [from_behind(): return lax.ppermute(block, axis, route)]
  transfers between devices with their start and end apart: 17 -> 16, of which waited for: 16 -> 16; matrix products, arithmetic and copies ran while one was open for 34% -> 23% of each run, Pallas kernels for 0% -> 0%
where the time goes in v1:
time: 556 us; the launch traced here: 551 us
  waiting for transfers between devices  310 us (56%)
  other arithmetic  89.6 us (16%)
  matrix products  56 us (10%)
  local copies, waits for them, and re-layouts  51.4 us (9%)
  blocking collectives  29.9 us (5%)
  between operations  13.5 us (2%)
    all_gather x1, waiting for transfers between devices, on_device(): lax.all_gather(jnp.concatenate([mean_agg, features], axis=0), 'bal', axis...  169 us
    ppermute x15, waiting for transfers between devices, from_behind(): return lax.ppermute(block, axis, route)  141 us
    scatter-add x16, other arithmetic, absorb(): return total.at[targets].add(masked)  75.4 us
    dot_general x16, matrix products, absorb(): jnp.einsum('sij,sjf->sif', vals, gathered, preferred_element_type=jnp.flo...  34.1 us
    all_to_all x1, blocking collectives, on_device(): lax.all_to_all(placed.astype(jnp.bfloat16).reshape(n_bal, capacity * TILE...  29.9 us
    another operation x15, local copies, waits for them, and re-layouts  18.4 us
    gather x16, local copies, waits for them, and re-layouts, absorb(): gathered = jnp.take(tiles, picks, axis=0)  11.8 us
    and x16, other arithmetic, absorb(): gathered = jnp.take(tiles, picks, axis=0)  11.2 us
  transfers between devices with their start and end apart: 16, of which 16 were waited for; matrix products, arithmetic and copies ran while one was open for 23% of the time, Pallas kernels for 0%

profile of v1, /device:TPU:0, one launch (start us, length us, event | category | flops | bytes accessed | tf_op | source)
XLA Modules:
  0.0 550.8 jit_solution(15338272817525731059)
XLA Ops:
  10.4 10.2 %fusion.43 = f32[1,16,32,128]{3,0,2,1:T(1,128)S(1)} fusion(bf16[1,16,32,128,128]{4,3,2,1,0:T(8,128)(2,1)} %param.14), kind=kOutput, calls=%fused_computation.73 | convolution fusion | flops 16777216 | bytes 17039360 | tf_op jit(solution)/shard_map/csij,j->csi/dot_general | solution.py:37
  22.1 287.5 %while.17 = (s32[]{:T(128)}, f32[64,128,64]{1,2,0:T(8,128)}, bf16[8192,64]{0,1:T(8,128)(2,1)}, s32[]{:T(128)}, s32[16,32]{1,0:T(8,128)S(1)}, /*index=5*/pred[16,...) while((s32[]{:T(128)}, f32[64,128,64]{1,2,0:T(8,128)}, ...), condition=%wide.region_4.6_spmd, body=%wide.region_2.5_spmd.sunk | while | flops 67896624 | bytes 15209832 | solution.py:61
  27.1 4.8 scatter_fusion
  31.9 9.4 %collective-permute-done = bf16[8192,64]{0,1:T(8,128)(2,1)} collective-permute-done((bf16[8192,64]{0,1:T(8,128)(2,1)S(1)}, bf16[8192,64]{0,1:T(8,128)(2,1)}, u32[]{:S(2)}, u32[]{:S(2)}) %collective-permute-start) | collective-permute-done | bytes 1048608 | tf_op jit(solution)/shard_map/while/body/eval_jaxpr/ppermute | solution.py:12
  46.3 4.8 scatter_fusion
  51.1 9.4 %collective-permute-done = bf16[8192,64]{0,1:T(8,128)(2,1)} collective-permute-done((bf16[8192,64]{0,1:T(8,128)(2,1)S(1)}, bf16[8192,64]{0,1:T(8,128)(2,1)}, u32[]{:S(2)}, u32[]{:S(2)}) %collective-permute-start) | collective-permute-done | bytes 1048608 | tf_op jit(solution)/shard_map/while/body/eval_jaxpr/ppermute | solution.py:12
  65.5 4.8 scatter_fusion
  70.3 9.4 %collective-permute-done = bf16[8192,64]{0,1:T(8,128)(2,1)} collective-permute-done((bf16[8192,64]{0,1:T(8,128)(2,1)S(1)}, bf16[8192,64]{0,1:T(8,128)(2,1)}, u32[]{:S(2)}, u32[]{:S(2)}) %collective-permute-start) | collective-permute-done | bytes 1048608 | tf_op jit(solution)/shard_map/while/body/eval_jaxpr/ppermute | solution.py:12
  84.6 4.8 scatter_fusion
  89.4 9.4 %collective-permute-done = bf16[8192,64]{0,1:T(8,128)(2,1)} collective-permute-done((bf16[8192,64]{0,1:T(8,128)(2,1)S(1)}, bf16[8192,64]{0,1:T(8,128)(2,1)}, u32[]{:S(2)}, u32[]{:S(2)}) %collective-permute-start) | collective-permute-done | bytes 1048608 | tf_op jit(solution)/shard_map/while/body/eval_jaxpr/ppermute | solution.py:12
  108.6 9.4 %collective-permute-done = bf16[8192,64]{0,1:T(8,128)(2,1)} collective-permute-done((bf16[8192,64]{0,1:T(8,128)(2,1)S(1)}, bf16[8192,64]{0,1:T(8,128)(2,1)}, u32[]{:S(2)}, u32[]{:S(2)}) %collective-permute-start) | collective-permute-done | bytes 1048608 | tf_op jit(solution)/shard_map/while/body/eval_jaxpr/ppermute | solution.py:12
  123.0 4.8 scatter_fusion
  127.8 9.4 %collective-permute-done = bf16[8192,64]{0,1:T(8,128)(2,1)} collective-permute-done((bf16[8192,64]{0,1:T(8,128)(2,1)S(1)}, bf16[8192,64]{0,1:T(8,128)(2,1)}, u32[]{:S(2)}, u32[]{:S(2)}) %collective-permute-start) | collective-permute-done | bytes 1048608 | tf_op jit(solution)/shard_map/while/body/eval_jaxpr/ppermute | solution.py:12
  142.2 4.8 scatter_fusion
  146.9 9.4 %collective-permute-done = bf16[8192,64]{0,1:T(8,128)(2,1)} collective-permute-done((bf16[8192,64]{0,1:T(8,128)(2,1)S(1)}, bf16[8192,64]{0,1:T(8,128)(2,1)}, u32[]{:S(2)}, u32[]{:S(2)}) %collective-permute-start) | collective-permute-done | bytes 1048608 | tf_op jit(solution)/shard_map/while/body/eval_jaxpr/ppermute | solution.py:12
  161.3 4.8 scatter_fusion
  166.1 9.4 %collective-permute-done = bf16[8192,64]{0,1:T(8,128)(2,1)} collective-permute-done((bf16[8192,64]{0,1:T(8,128)(2,1)S(1)}, bf16[8192,64]{0,1:T(8,128)(2,1)}, u32[]{:S(2)}, u32[]{:S(2)}) %collective-permute-start) | collective-permute-done | bytes 1048608 | tf_op jit(solution)/shard_map/while/body/eval_jaxpr/ppermute | solution.py:12
  180.5 4.8 scatter_fusion
  185.3 9.4 %collective-permute-done = bf16[8192,64]{0,1:T(8,128)(2,1)} collective-permute-done((bf16[8192,64]{0,1:T(8,128)(2,1)S(1)}, bf16[8192,64]{0,1:T(8,128)(2,1)}, u32[]{:S(2)}, u32[]{:S(2)}) %collective-permute-start) | collective-permute-done | bytes 1048608 | tf_op jit(solution)/shard_map/while/body/eval_jaxpr/ppermute | solution.py:12
  199.7 4.8 scatter_fusion
  204.4 9.4 %collective-permute-done = bf16[8192,64]{0,1:T(8,128)(2,1)} collective-permute-done((bf16[8192,64]{0,1:T(8,128)(2,1)S(1)}, bf16[8192,64]{0,1:T(8,128)(2,1)}, u32[]{:S(2)}, u32[]{:S(2)}) %collective-permute-start) | collective-permute-done | bytes 1048608 | tf_op jit(solution)/shard_map/while/body/eval_jaxpr/ppermute | solution.py:12
  218.8 4.8 scatter_fusion
  223.6 9.4 %collective-permute-done = bf16[8192,64]{0,1:T(8,128)(2,1)} collective-permute-done((bf16[8192,64]{0,1:T(8,128)(2,1)S(1)}, bf16[8192,64]{0,1:T(8,128)(2,1)}, u32[]{:S(2)}, u32[]{:S(2)}) %collective-permute-start) | collective-permute-done | bytes 1048608 | tf_op jit(solution)/shard_map/while/body/eval_jaxpr/ppermute | solution.py:12
  238.0 4.8 scatter_fusion
  242.8 9.4 %collective-permute-done = bf16[8192,64]{0,1:T(8,128)(2,1)} collective-permute-done((bf16[8192,64]{0,1:T(8,128)(2,1)S(1)}, bf16[8192,64]{0,1:T(8,128)(2,1)}, u32[]{:S(2)}, u32[]{:S(2)}) %collective-permute-start) | collective-permute-done | bytes 1048608 | tf_op jit(solution)/shard_map/while/body/eval_jaxpr/ppermute | solution.py:12
  261.9 9.4 %collective-permute-done = bf16[8192,64]{0,1:T(8,128)(2,1)} collective-permute-done((bf16[8192,64]{0,1:T(8,128)(2,1)S(1)}, bf16[8192,64]{0,1:T(8,128)(2,1)}, u32[]{:S(2)}, u32[]{:S(2)}) %collective-permute-start) | collective-permute-done | bytes 1048608 | tf_op jit(solution)/shard_map/while/body/eval_jaxpr/ppermute | solution.py:12
  281.1 9.4 %collective-permute-done = bf16[8192,64]{0,1:T(8,128)(2,1)} collective-permute-done((bf16[8192,64]{0,1:T(8,128)(2,1)S(1)}, bf16[8192,64]{0,1:T(8,128)(2,1)}, u32[]{:S(2)}, u32[]{:S(2)}) %collective-permute-start) | collective-permute-done | bytes 1048608 | tf_op jit(solution)/shard_map/while/body/eval_jaxpr/ppermute | solution.py:12
  300.3 9.4 %collective-permute-done = bf16[8192,64]{0,1:T(8,128)(2,1)} collective-permute-done((bf16[8192,64]{0,1:T(8,128)(2,1)S(1)}, bf16[8192,64]{0,1:T(8,128)(2,1)}, u32[]{:S(2)}, u32[]{:S(2)}) %collective-permute-start) | collective-permute-done | bytes 1048608 | tf_op jit(solution)/shard_map/while/body/eval_jaxpr/ppermute | solution.py:12
  326.1 169.0 %all-gather.2.cloned.1.call-done = bf16[16384,512]{0,1:T(8,128)(2,1)} async-done(((bf16[16384,64]{0,1:T(8,128)(2,1)}), bf16[16384,512]{0,1:T(8,128)(2,1)}) %all-gather.2.cloned.1.call-update) | async-done | bytes 16777232 | tf_op jit(solution)/shard_map/all_gather | solution.py:74
  495.1 5.1 fusion.14
  500.2 5.2 fusion.16
  511.5 29.9 %all_to_all.15 = bf16[8,2048,64]{1,2,0:T(8,128)(2,1)S(1)} all-to-all(bf16[8,2048,64]{1,2,0:T(8,128)(2,1)S(1)} %copy.17), channel_id=1, replica_groups=mesh['blk'=16,'bal'=8] {'bal'}, dimensions={0} | all-to-all | bytes 4194304 | tf_op jit(solution)/shard_map/all_to_all | solution.py:87
  (175 shorter events, 124.0 us)
Async XLA Ops:
  6.5 488.5 %copy-start = (bf16[512,512]{1,0:T(8,128)(2,1)S(1)}, bf16[512,512]{1,0:T(8,128)(2,1)}, u32[]{:S(2)}) copy-start(bf16[512,512]{1,0:T(8,128)(2,1)} %param.19) | copy-start | bytes 1572868
  6.5 3.8 copy-start.4
  6.5 488.5 %all-gather.2.cloned.1.call-start = ((), (), s32[]{:S(2)}) async-start(), calls=%async_computation.1 | async-start | bytes 18874368 | tf_op jit(solution)/shard_map/all_gather | solution.py:74
  23.4 17.9 %collective-permute-start = (bf16[8192,64]{0,1:T(8,128)(2,1)S(1)}, bf16[8192,64]{0,1:T(8,128)(2,1)}, u32[]{:S(2)}, u32[]{:S(2)}) collective-permute-start(bf16[8192,64]{0,1:T(8,128)(2,1)S(1)} %copy.36), channel_id=1, source_target_pairs={{120,0},{0,8},{8,16},{16,24},{24,32},{32,40},{40,48},{48,56},{56,6... | collective-permute-start | bytes 3145736 | tf_op jit(solution)/shard_map/while/body/eval_jaxpr/ppermute | solution.py:12
  42.5 17.9 %collective-permute-start = (bf16[8192,64]{0,1:T(8,128)(2,1)S(1)}, bf16[8192,64]{0,1:T(8,128)(2,1)}, u32[]{:S(2)}, u32[]{:S(2)}) collective-permute-start(bf16[8192,64]{0,1:T(8,128)(2,1)S(1)} %copy.36), channel_id=1, source_target_pairs={{120,0},{0,8},{8,16},{16,24},{24,32},{32,40},{40,48},{48,56},{56,6... | collective-permute-start | bytes 3145736 | tf_op jit(solution)/shard_map/while/body/eval_jaxpr/ppermute | solution.py:12
  61.7 17.9 %collective-permute-start = (bf16[8192,64]{0,1:T(8,128)(2,1)S(1)}, bf16[8192,64]{0,1:T(8,128)(2,1)}, u32[]{:S(2)}, u32[]{:S(2)}) collective-permute-start(bf16[8192,64]{0,1:T(8,128)(2,1)S(1)} %copy.36), channel_id=1, source_target_pairs={{120,0},{0,8},{8,16},{16,24},{24,32},{32,40},{40,48},{48,56},{56,6... | collective-permute-start | bytes 3145736 | tf_op jit(solution)/shard_map/while/body/eval_jaxpr/ppermute | solution.py:12
  80.9 17.9 %collective-permute-start = (bf16[8192,64]{0,1:T(8,128)(2,1)S(1)}, bf16[8192,64]{0,1:T(8,128)(2,1)}, u32[]{:S(2)}, u32[]{:S(2)}) collective-permute-start(bf16[8192,64]{0,1:T(8,128)(2,1)S(1)} %copy.36), channel_id=1, source_target_pairs={{120,0},{0,8},{8,16},{16,24},{24,32},{32,40},{40,48},{48,56},{56,6... | collective-permute-start | bytes 3145736 | tf_op jit(solution)/shard_map/while/body/eval_jaxpr/ppermute | solution.py:12
  100.0 17.9 %collective-permute-start = (bf16[8192,64]{0,1:T(8,128)(2,1)S(1)}, bf16[8192,64]{0,1:T(8,128)(2,1)}, u32[]{:S(2)}, u32[]{:S(2)}) collective-permute-start(bf16[8192,64]{0,1:T(8,128)(2,1)S(1)} %copy.36), channel_id=1, source_target_pairs={{120,0},{0,8},{8,16},{16,24},{24,32},{32,40},{40,48},{48,56},{56,6... | collective-permute-start | bytes 3145736 | tf_op jit(solution)/shard_map/while/body/eval_jaxpr/ppermute | solution.py:12
  119.2 17.9 %collective-permute-start = (bf16[8192,64]{0,1:T(8,128)(2,1)S(1)}, bf16[8192,64]{0,1:T(8,128)(2,1)}, u32[]{:S(2)}, u32[]{:S(2)}) collective-permute-start(bf16[8192,64]{0,1:T(8,128)(2,1)S(1)} %copy.36), channel_id=1, source_target_pairs={{120,0},{0,8},{8,16},{16,24},{24,32},{32,40},{40,48},{48,56},{56,6... | collective-permute-start | bytes 3145736 | tf_op jit(solution)/shard_map/while/body/eval_jaxpr/ppermute | solution.py:12
  138.4 17.9 %collective-permute-start = (bf16[8192,64]{0,1:T(8,128)(2,1)S(1)}, bf16[8192,64]{0,1:T(8,128)(2,1)}, u32[]{:S(2)}, u32[]{:S(2)}) collective-permute-start(bf16[8192,64]{0,1:T(8,128)(2,1)S(1)} %copy.36), channel_id=1, source_target_pairs={{120,0},{0,8},{8,16},{16,24},{24,32},{32,40},{40,48},{48,56},{56,6... | collective-permute-start | bytes 3145736 | tf_op jit(solution)/shard_map/while/body/eval_jaxpr/ppermute | solution.py:12
  157.5 17.9 %collective-permute-start = (bf16[8192,64]{0,1:T(8,128)(2,1)S(1)}, bf16[8192,64]{0,1:T(8,128)(2,1)}, u32[]{:S(2)}, u32[]{:S(2)}) collective-permute-start(bf16[8192,64]{0,1:T(8,128)(2,1)S(1)} %copy.36), channel_id=1, source_target_pairs={{120,0},{0,8},{8,16},{16,24},{24,32},{32,40},{40,48},{48,56},{56,6... | collective-permute-start | bytes 3145736 | tf_op jit(solution)/shard_map/while/body/eval_jaxpr/ppermute | solution.py:12
  176.7 17.9 %collective-permute-start = (bf16[8192,64]{0,1:T(8,128)(2,1)S(1)}, bf16[8192,64]{0,1:T(8,128)(2,1)}, u32[]{:S(2)}, u32[]{:S(2)}) collective-permute-start(bf16[8192,64]{0,1:T(8,128)(2,1)S(1)} %copy.36), channel_id=1, source_target_pairs={{120,0},{0,8},{8,16},{16,24},{24,32},{32,40},{40,48},{48,56},{56,6... | collective-permute-start | bytes 3145736 | tf_op jit(solution)/shard_map/while/body/eval_jaxpr/ppermute | solution.py:12
  195.9 17.9 %collective-permute-start = (bf16[8192,64]{0,1:T(8,128)(2,1)S(1)}, bf16[8192,64]{0,1:T(8,128)(2,1)}, u32[]{:S(2)}, u32[]{:S(2)}) collective-permute-start(bf16[8192,64]{0,1:T(8,128)(2,1)S(1)} %copy.36), channel_id=1, source_target_pairs={{120,0},{0,8},{8,16},{16,24},{24,32},{32,40},{40,48},{48,56},{56,6... | collective-permute-start | bytes 3145736 | tf_op jit(solution)/shard_map/while/body/eval_jaxpr/ppermute | solution.py:12
  215.1 17.9 %collective-permute-start = (bf16[8192,64]{0,1:T(8,128)(2,1)S(1)}, bf16[8192,64]{0,1:T(8,128)(2,1)}, u32[]{:S(2)}, u32[]{:S(2)}) collective-permute-start(bf16[8192,64]{0,1:T(8,128)(2,1)S(1)} %copy.36), channel_id=1, source_target_pairs={{120,0},{0,8},{8,16},{16,24},{24,32},{32,40},{40,48},{48,56},{56,6... | collective-permute-start | bytes 3145736 | tf_op jit(solution)/shard_map/while/body/eval_jaxpr/ppermute | solution.py:12
  234.2 17.9 %collective-permute-start = (bf16[8192,64]{0,1:T(8,128)(2,1)S(1)}, bf16[8192,64]{0,1:T(8,128)(2,1)}, u32[]{:S(2)}, u32[]{:S(2)}) collective-permute-start(bf16[8192,64]{0,1:T(8,128)(2,1)S(1)} %copy.36), channel_id=1, source_target_pairs={{120,0},{0,8},{8,16},{16,24},{24,32},{32,40},{40,48},{48,56},{56,6... | collective-permute-start | bytes 3145736 | tf_op jit(solution)/shard_map/while/body/eval_jaxpr/ppermute | solution.py:12
  253.4 17.9 %collective-permute-start = (bf16[8192,64]{0,1:T(8,128)(2,1)S(1)}, bf16[8192,64]{0,1:T(8,128)(2,1)}, u32[]{:S(2)}, u32[]{:S(2)}) collective-permute-start(bf16[8192,64]{0,1:T(8,128)(2,1)S(1)} %copy.36), channel_id=1, source_target_pairs={{120,0},{0,8},{8,16},{16,24},{24,32},{32,40},{40,48},{48,56},{56,6... | collective-permute-start | bytes 3145736 | tf_op jit(solution)/shard_map/while/body/eval_jaxpr/ppermute | solution.py:12
  272.6 17.9 %collective-permute-start = (bf16[8192,64]{0,1:T(8,128)(2,1)S(1)}, bf16[8192,64]{0,1:T(8,128)(2,1)}, u32[]{:S(2)}, u32[]{:S(2)}) collective-permute-start(bf16[8192,64]{0,1:T(8,128)(2,1)S(1)} %copy.36), channel_id=1, source_target_pairs={{120,0},{0,8},{8,16},{16,24},{24,32},{32,40},{40,48},{48,56},{56,6... | collective-permute-start | bytes 3145736 | tf_op jit(solution)/shard_map/while/body/eval_jaxpr/ppermute | solution.py:12
  291.7 17.9 %collective-permute-start = (bf16[8192,64]{0,1:T(8,128)(2,1)S(1)}, bf16[8192,64]{0,1:T(8,128)(2,1)}, u32[]{:S(2)}, u32[]{:S(2)}) collective-permute-start(bf16[8192,64]{0,1:T(8,128)(2,1)S(1)} %copy.36), channel_id=1, source_target_pairs={{120,0},{0,8},{8,16},{16,24},{24,32},{32,40},{40,48},{48,56},{56,6... | collective-permute-start | bytes 3145736 | tf_op jit(solution)/shard_map/while/body/eval_jaxpr/ppermute | solution.py:12
  312.8 5.1 copy-start.1
  321.6 1.2 copy-start.2
  324.3 0.7 copy-start.3
Sparse Core Ops, SparseCore 0:
  324.5 170.5 all-gather.1
